TPU v7x, 256 devices: a whole 4x4x8 slice. The times are simulated.
256 devices in a mesh: reg: 64 (over z, y, core), ep: 4 (over x).
Axes of the slice: x: 4, y: 4, z: 8, core: 2. Of those that a mesh axis runs over, the one named last changes fastest.
Arguments:
- log_prices: bfloat16 [256, 64, 256], P('reg', 'ep'), may hold values from -3 to 3
- log_wages: float32 [256, 64], P('reg', 'ep'), may hold values from -12 to 1
- labor_share: float32 [256, 256], P('reg'), may hold values from 0.3 to 0.7
- io_coeffs: bfloat16 [256, 256, 256], P('reg'), may hold values from -0.375 to 0.375
- pair_blocks: bfloat16 [256, 32, 256, 256], P('reg'), may hold values from -0.0201 to 0.801
- log_tau: float32 [256, 32, 256], P('reg'), may hold values from 0.05 to 2
- elasticity: float32 [256], replicated, may hold values from 2 to 40
- partners: int32 [256, 32], replicated, may hold values from 0 to 255, as said below
- list_lengths: int32 [256], replicated, may hold values from 1 to 32, as said below
- price_cotangent: float32 [256, 64, 256], P('reg', 'ep'), may hold values from -6 to 6
Outputs:
- new_prices: bfloat16 [256, 64, 256], P('reg', 'ep')
- price_grad: float32 [256, 64, 256], P('reg', 'ep')
- wage_grad: float32 [256, 64], P('reg', 'ep')
- tau_grad: float32 [256, 32, 256], P('reg')
Inputs may be any that keep to these rules, and one draw needn't show every extreme that they name: `partners`: each list names distinct regions. Over their live entries, the 4 importers of an aligned block name at most 2 regions of any one aligned block of 4 regions, and this is reached in every draw. `list_lengths`: in some aligned block of 4 regions every list has 32 live entries.
All inputs are finite; a program needn't handle non-finite values.
Results may differ from a plain program's by a relative error of at most 0.0064.
Values may be sent and summed in bfloat16 or wider, within the bound.
A program may use at most 64 MiB of HBM per device.

v0:
```python
import jax
import jax.numpy as jnp
from jax import lax
from jax.sharding import PartitionSpec as P


def shards(
    log_prices,
    log_wages,
    labor_share,
    io_coeffs,
    pair_blocks,
    log_tau,
    elasticity,
    partners,
    list_lengths,
    price_cotangent,
):
    own_regions, episodes, sectors = log_prices.shape
    max_slots = pair_blocks.shape[1]
    slot_total = own_regions * max_slots
    row_width = episodes * sectors
    my_index = lax.axis_index("reg")
    unit_cost = (
        labor_share[:, None, :] * log_wages[:, :, None]
        + jnp.einsum("iek,ikj->iej", log_prices, io_coeffs, preferred_element_type=jnp.float32)
    ).astype(jnp.bfloat16)
    first_region = my_index * own_regions
    my_partners = lax.dynamic_slice_in_dim(partners, first_region, own_regions, 0)
    my_lengths = lax.dynamic_slice_in_dim(list_lengths, first_region, own_regions, 0)
    slot_index = jnp.arange(max_slots, dtype=jnp.int32)
    live = slot_index[None, :] < my_lengths[:, None]
    flat_partners = my_partners.reshape(-1)
    shard_rows = lax.all_gather(unit_cost, "reg", axis=0, tiled=True)
    row_count = shard_rows.shape[0]
    selector = (flat_partners[:, None] == jnp.arange(row_count, dtype=jnp.int32)[None, :]).astype(
        jnp.bfloat16
    )
    exporter_rows = jnp.dot(
        selector, shard_rows.reshape(row_count, row_width), preferred_element_type=jnp.float32
    ).astype(jnp.bfloat16)
    exporter_rows = exporter_rows.reshape(own_regions, max_slots, episodes, sectors)
    landed = log_tau[:, :, None, :] + jnp.einsum(
        "rsek,rskj->rsej", exporter_rows, pair_blocks, preferred_element_type=jnp.float32
    )
    live_mask = live[:, :, None, None]
    scores = jnp.where(live_mask, -elasticity * landed, -jnp.inf)
    top_score = jnp.max(scores, axis=1)
    weights = jnp.exp(scores - top_score[:, None])
    total = jnp.sum(weights, axis=1)
    new_prices = (-(top_score + jnp.log(total)) / elasticity).astype(jnp.bfloat16)
    adjoint = price_cotangent[:, None] * (weights / total[:, None])
    tau_grad = lax.psum(jnp.sum(adjoint, axis=2), "ep")
    pushed = jnp.einsum(
        "rsej,rskj->rsek",
        adjoint.astype(jnp.bfloat16),
        pair_blocks,
        preferred_element_type=jnp.float32,
    ).astype(jnp.bfloat16)
    pushed = jnp.where(live_mask, pushed, jnp.zeros((), jnp.bfloat16)).reshape(
        slot_total, row_width
    )
    selector = (
        jnp.arange(own_regions * lax.axis_size("reg"), dtype=jnp.int32)[:, None]
        == flat_partners[None, :]
    ).astype(jnp.bfloat16)
    cost_adjoint = lax.psum_scatter(
        jnp.dot(selector, pushed, preferred_element_type=jnp.float32),
        "reg",
        scatter_dimension=0,
        tiled=True,
    )
    cost_adjoint = cost_adjoint.reshape(own_regions, episodes, sectors)
    price_grad = jnp.einsum(
        "iej,ikj->iek",
        cost_adjoint.astype(jnp.bfloat16),
        io_coeffs,
        preferred_element_type=jnp.float32,
    )
    wage_grad = jnp.sum(cost_adjoint * labor_share[:, None, :], axis=2)
    return (new_prices, price_grad, wage_grad, tau_grad)


def solution(mesh):
    return jax.shard_map(
        shards,
        mesh=mesh,
        in_specs=(
            P("reg", "ep", None),
            P("reg", "ep"),
            P("reg", None),
            P("reg", None, None),
            P("reg", None, None, None),
            P("reg", None, None),
            P(),
            P(),
            P(),
            P("reg", "ep", None),
        ),
        out_specs=(
            P("reg", "ep", None),
            P("reg", "ep", None),
            P("reg", "ep"),
            P("reg", None, None),
        ),
        check_vma=False,
    )
```

profile of v0, /device:TPU:8, one launch (start us, length us, event | category | flops | bytes accessed | tf_op | source)
XLA Modules:
  0.0 369.9 jit_solution(17830627746724783566)
XLA Ops:
  7.2 1.0 copy-done
  8.2 1.6 fusion.2
  9.9 0.7 neg.6
  10.6 0.8 dynamic_slice.6
  11.3 0.8 constant_dynamic-slice_fusion.1
  12.3 78.3 %all-gather.2.cloned.1.call-done = bf16[256,16,256]{2,1,0:T(8,128)(2,1)} async-done(((bf16[4,16,256]{2,1,0:T(8,128)(2,1)}), bf16[256,16,256]{2,1,0:T(8,128)(2,1)}) %all-gather.2.cloned.1.call-update) | async-done | bytes 2097168 | tf_op jit(solution)/shard_map/all_gather | solution.py:34
  90.6 2.5 copy.16
  93.2 0.5 convolution_convert_fusion
  94.1 8.1 %fusion.11 = (f32[4,16,256]{2,1,0:T(8,128)S(1)}, f32[4,32,16,256]{3,2,1,0:T(8,128)S(1)}) fusion(bf16[4,32,256,256]{3,2,1,0:T(8,128)(2,1)} %param.14, f32[4,32,256]{2,1,0:T(8,128)S(1)} %copy-done.2, f32[256]{0:T(256)S(1)} %neg.6, pred[4,32]{1,0:T(4,128)(4,1)S(1)} %iota_compare_fusion.4, bf16[4,32,16,256]{3,2,1,0:T(8,128)(2,1)S(1)} %bitcast.31), kind=kOutput, calls=%fused_computation.25 | convolution fusion | flops 270516224 | bytes 20120704 | tf_op jit(solution)/shard_map/rsek,rskj->rsej/dot_general | solution.py:43
  102.2 0.3 fusion
  102.5 0.5 copy-done.1
  103.1 11.2 %fusion.1 = bf16[4,32,16,256]{3,2,1,0:T(8,128)(2,1)} fusion(bf16[4,32,256,256]{3,2,1,0:T(8,128)(2,1)} %param.14, pred[4,32]{1,0:T(4,128)(4,1)S(1)} %iota_compare_fusion.4, f32[4,32,16,256]{3,2,1,0:T(8,128)S(1)} %get-tuple-element.5, f32[4,16,256]{2,1,0:T(8,128)S(1)} %fusion, f32[4,16,256]{2,1,0:T(8,128)S(1)} %copy-done.1, f32[4,16,256]{2,1,0:T(8,128)S(1)} %get-tuple-element.4), kind=kOutput, calls=%fused_computation.6 | convolution fusion | flops 271581184 | bytes 20119680 | tf_op jit(solution)/shard_map/rsej,rskj->rsek/dot_general | solution.py:54
  114.3 1.6 copy.18
  116.0 2.7 fusion.6
  118.7 0.6 copy-done.5
  119.3 0.6 dynamic-slice
  120.5 0.6 divide_convert_fusion
  121.2 1.3 fusion.5
  122.5 191.0 %all-reduce.6.cloned.1.call-done = f32[256,4096]{1,0:T(8,128)} async-done(((f32[256,4096]{1,0:T(8,128)}), f32[256,4096]{1,0:T(8,128)}) %all-reduce.6.cloned.1.call-update) | async-done | bytes 4194320
  313.5 0.9 constant_dynamic-slice_fusion
  314.5 0.9 fusion.10
  315.4 0.7 fusion.7
  316.0 45.7 %all-reduce.4.cloned.1.call-done = f32[4,32,256]{2,1,0:T(8,128)} async-done(((f32[4,32,256]{2,1,0:T(8,128)}), f32[4,32,256]{2,1,0:T(8,128)}) %all-reduce.4.cloned.1.call-update) | async-done | bytes 131088 | tf_op jit(solution)/shard_map/psum | solution.py:53
  361.8 1.6 copy.25
  (19 shorter events, 0.8 us)
Async XLA Ops:
  7.2 1.0 copy-start
  7.2 83.5 %all-gather.2.cloned.1.call-start = ((), (), s32[]{:S(2)}) async-start(), calls=%async_computation | async-start | bytes 2129920 | tf_op jit(solution)/shard_map/all_gather | solution.py:34
  9.8 303.7 %all-reduce.6.cloned.1.call-start = ((), (), s32[]{:S(2)}) async-start(), calls=%async_computation.2 | async-start | bytes 8388608
  93.2 0.9 copy-start.2
  102.2 0.8 copy-start.1
  118.6 0.7 copy-start.5
  118.6 1.9 copy-start.4
  118.7 196.7 %copy-start.3 = (f32[4,256]{1,0:T(4,128)S(1)}, f32[4,256]{1,0:T(4,128)}, u32[]{:S(2)}) copy-start(f32[4,256]{1,0:T(4,128)} %param.12) | copy-start | bytes 12292
  118.7 243.1 %all-reduce.4.cloned.1.call-start = ((), (), s32[]{:S(2)}) async-start(), calls=%async_computation.1 | async-start | bytes 262144 | tf_op jit(solution)/shard_map/psum | solution.py:53
Sparse Core Ops, SparseCore 0:
  11.3 79.2 all-gather.1
  118.8 194.7 all-reduce.5
  316.4 45.2 all-reduce.3
where the time goes:
time: 370 us
  waiting for transfers between devices  315 us (85%)
  matrix products  25 us (7%)
  between operations  14.5 us (4%)
  local copies, waits for them, and re-layouts  11.5 us (3%)
    unnamed x4, waiting for transfers between devices  191 us
    all_gather x1, waiting for transfers between devices, shards(): shard_rows = lax.all_gather(unit_cost, 'reg', axis=0, tiled=True)  78.3 us
    psum x1, waiting for transfers between devices, shards(): tau_grad = lax.psum(jnp.sum(adjoint, axis=2), 'ep')  45.7 us
    dot_general x1, matrix products, shards(): jnp.einsum('rsej,rskj->rsek', adjoint.astype(jnp.bfloat16), pair_blocks,...  11.2 us
    unnamed x18, local copies, waits for them, and re-layouts  9.77 us
    dot_general x1, matrix products, shards(): jnp.einsum('rsek,rskj->rsej', exporter_rows, pair_blocks, preferred_eleme...  8.14 us
  transfers between devices with their start and end apart: 3, of which 3 were waited for; matrix products, arithmetic and copies ran while one was open for 2% of the time, Pallas kernels for 0%

commit v1 on v0

v1 whole, which is shorter than its diff:
```python
import jax
import jax.numpy as jnp
from jax import lax
from jax.experimental import pallas as pl
from jax.experimental.pallas import tpu as pltpu
from jax.sharding import PartitionSpec as P

NZ, NY, NC = 8, 4, 2
OUT = (0, 1, 7, 2, 6, 3, 5, 4)
F32 = jnp.float32
BF16 = jnp.bfloat16
MESH = pl.DeviceIdType.MESH
VMEM = pl.BlockSpec(memory_space=pltpu.VMEM)
ANY = pl.BlockSpec(memory_space=pl.ANY)
DMA = pltpu.SemaphoreType.DMA


def place():
    me = lax.axis_index("reg")
    return me // (NY * NC), (me // NC) % NY, me % NC


def at(z, y, c):
    return {"reg": (z * NY + y) * NC + c}


def greet(z, y, c, across):
    barrier = pltpu.get_barrier_semaphore()
    peers = [at((z + d) % NZ, y, c) for d in range(1, NZ)]
    peers += [at(z, (y + 1) % NY, c), at(z, (y + NY - 1) % NY, c), at(z, y, 1 - c)]
    if across:
        here = lax.axis_index("ep")
        size = lax.axis_size("ep")
        peers += [{"ep": (here + d) % size} for d in range(1, size)]
    for peer in peers:
        pl.semaphore_signal(barrier, inc=1, device_id=peer, device_id_type=MESH)
    return barrier, len(peers)


def gather_kernel(
    prices, wages, share, io, rows,
    z_send, z_recv, y_send, y_recv, h_send, h_recv, c_send, c_recv,
):
    z, y, c = place()
    right, left, across = (y + 1) % NY, (y + NY - 1) % NY, (y + 2) % NY
    barrier, count = greet(z, y, c, False)
    episodes = prices.shape[1]
    eye = lax.broadcasted_iota(jnp.int32, (episodes, episodes), 0) == lax.broadcasted_iota(
        jnp.int32, (episodes, episodes), 1
    )
    for i in range(prices.shape[0]):
        column = jnp.sum(
            jnp.where(eye, wages[i : i + 1, :], 0.0), axis=1, keepdims=True
        )
        cost = column * share[i : i + 1, :] + jnp.dot(
            prices[i], io[i], preferred_element_type=F32
        )
        rows[z, y, c, i] = cost.astype(BF16)
    pl.semaphore_wait(barrier, count)

    def copy(block, ssem, rsem, dev):
        return pltpu.make_async_remote_copy(
            src_ref=block, dst_ref=block, send_sem=ssem, recv_sem=rsem,
            device_id=dev, device_id_type=MESH,
        )

    sends = []

    def go(block, ssem, rsem, dev):
        one = copy(block, ssem, rsem, dev)
        one.start()
        sends.append(one)

    own = rows.at[z, y, c]
    go(own, y_send.at[0, 0], y_recv.at[0, 0], at(z, right, c))
    go(own, y_send.at[0, 1], y_recv.at[0, 1], at(z, left, c))
    for d in OUT[1:]:
        go(own, z_send.at[d], z_recv.at[d], at((z + d) % NZ, y, c))
    half = prices.shape[0] // 2
    for t in range(NZ + 2):
        if 0 < t < NZ:
            d = OUT[t]
            zz = (z + NZ - d) % NZ
            block = rows.at[zz, y, c]
            copy(block, z_send.at[d], z_recv.at[d], at(z, y, c)).wait_recv()
            go(block, y_send.at[t, 0], y_recv.at[t, 0], at(z, right, c))
            go(block, y_send.at[t, 1], y_recv.at[t, 1], at(z, left, c))
        if 0 < t < NZ + 1:
            k = t - 1
            zz = (z + NZ - OUT[k]) % NZ
            block = rows.at[zz, left, c]
            copy(block, y_send.at[k, 0], y_recv.at[k, 0], at(z, y, c)).wait_recv()
            go(block.at[:half], h_send.at[k, 0], h_recv.at[k, 0], at(z, right, c))
            block = rows.at[zz, right, c]
            copy(block, y_send.at[k, 1], y_recv.at[k, 1], at(z, y, c)).wait_recv()
            go(block.at[half:], h_send.at[k, 1], h_recv.at[k, 1], at(z, left, c))
        if t > 1:
            k = t - 2
            zz = (z + NZ - OUT[k]) % NZ
            block = rows.at[zz, across, c]
            copy(block.at[:half], h_send.at[k, 0], h_recv.at[k, 0], at(z, y, c)).wait_recv()
            copy(block.at[half:], h_send.at[k, 1], h_recv.at[k, 1], at(z, y, c)).wait_recv()
            go(rows.at[zz, :, c], c_send.at[k], c_recv.at[k], at(z, y, 1 - c))
    for k in range(NZ):
        zz = (z + NZ - OUT[k]) % NZ
        copy(rows.at[zz, :, 1 - c], c_send.at[k], c_recv.at[k], at(z, y, c)).wait_recv()
    for one in sends:
        one.wait_send()


def slots_kernel(
    rows, blocks, tau, elasticity, partners, lengths, cotangent,
    prices_out, tau_out, pushed_out,
    weights, held, who, how, adjoint, b_sem, w_sem,
):
    regions, slots = blocks.shape[0], blocks.shape[1]
    episodes, sectors = cotangent.shape[1], cotangent.shape[2]
    step = slots // held_chunks(slots)
    chunks = slots // step
    me = lax.axis_index("reg")
    base = (me // 2) * 8
    inner = (me % 2) * regions
    copies = [
        pltpu.make_async_copy(partners.at[pl.ds(pl.multiple_of(base, 8), 8)], who, w_sem.at[0]),
        pltpu.make_async_copy(lengths, how, w_sem.at[1]),
    ]
    for one in copies:
        one.start()
    for n in range(regions):
        for q in range(chunks):
            part = pl.ds(q * step, step)
            pltpu.make_async_copy(
                blocks.at[n, part], held.at[n, part], b_sem.at[n * chunks + q]
            ).start()
    pushed_out[...] = jnp.zeros_like(pushed_out)
    for one in copies:
        one.wait()
    slope = -elasticity[...]
    for n in range(regions):
        length = how[me * regions + n]
        top = jnp.full((episodes, sectors), -jnp.inf, F32)
        for q in range(chunks):
            part = pl.ds(q * step, step)
            pltpu.make_async_copy(
                blocks.at[n, part], held.at[n, part], b_sem.at[n * chunks + q]
            ).wait()

            for s in range(q * step, (q + 1) * step):
                landed = tau[n, s : s + 1, :] + jnp.dot(
                    rows[who[inner + n, s]], held[n, s], preferred_element_type=F32
                )
                score = jnp.where(s < length, slope * landed, -jnp.inf)
                weights[s] = score
                top = jnp.maximum(top, score)
        total = jnp.zeros((episodes, sectors), F32)
        for s in range(slots):
            one = jnp.exp(weights[s] - top)
            weights[s] = one
            total = total + one
        prices_out[n] = (-(top + jnp.log(total)) / elasticity[...]).astype(BF16)
        scale = cotangent[n] / total
        for s in range(slots):
            one = weights[s] * scale
            tau_out[n, s : s + 1, :] = jnp.sum(one, axis=0, keepdims=True)
            pushed = lax.dot_general(
                one.astype(BF16), held[n, s], (((1,), (1,)), ((), ())),
                preferred_element_type=F32,
            ).astype(BF16)
            row = who[inner + n, s]
            pushed_out[row] = (pushed_out[row].astype(F32) + pushed.astype(F32)).astype(BF16)


def held_chunks(slots):
    return 4


def scatter_kernel(
    pushed, tau, share, io,
    price_grad, wage_grad, tau_grad,
    from_core, far, near, mine, a_recv, b_recv, z_in, x_in,
    c_send, c_recv, a_send, a_rsem, b_send, b_rsem, z_send, z_rsem, x_send, x_rsem,
):
    z, y, c = place()
    right, left, across = (y + 1) % NY, (y + NY - 1) % NY, (y + 2) % NY
    here = lax.axis_index("ep")
    size = lax.axis_size("ep")
    barrier, count = greet(z, y, c, True)
    pl.semaphore_wait(barrier, count)
    half = pushed.shape[3] // 2
    sends = []

    def copy(src, dst, ssem, rsem, dev):
        return pltpu.make_async_remote_copy(
            src_ref=src, dst_ref=dst, send_sem=ssem, recv_sem=rsem,
            device_id=dev, device_id_type=MESH,
        )

    def go(*args):
        one = copy(*args)
        one.start()
        sends.append(one)
        return one

    order = OUT[::-1]
    arrivals = []
    for k in range(NZ):
        zz = (z + order[k]) % NZ
        arrivals.append(
            go(pushed.at[zz, :, 1 - c], from_core.at[k], c_send.at[k], c_recv.at[k], at(z, y, 1 - c))
        )
    tau_moves = [
        go(tau, x_in.at[here], x_send.at[d], x_rsem.at[d], {"ep": (here + d) % size})
        for d in range(1, size)
    ]
    x_in[here] = tau[...]

    def chip(k, yy, part):
        zz = (z + order[k]) % NZ
        return pushed[zz, yy, c, part].astype(F32) + from_core[k, yy, part].astype(F32)

    lo, hi, whole = pl.ds(0, half), pl.ds(half, half), pl.ds(0, 2 * half)
    a_moves, b_moves, z_moves = {}, {}, {}
    for t in range(NZ + 2):
        if t < NZ:
            k = t
            arrivals[k].wait_recv()
            far[k] = chip(k, across, whole).astype(BF16)
            a_moves[k] = (
                go(far.at[k, lo], a_recv.at[k, 0], a_send.at[k, 0], a_rsem.at[k, 0], at(z, right, c)),
                go(far.at[k, hi], a_recv.at[k, 1], a_send.at[k, 1], a_rsem.at[k, 1], at(z, left, c)),
            )
        if 0 < t < NZ + 1:
            k = t - 1
            a_moves[k][0].wait_recv()
            near[k, 0, lo] = (chip(k, right, lo) + a_recv[k, 0].astype(F32)).astype(BF16)
            near[k, 0, hi] = chip(k, right, hi).astype(BF16)
            a_moves[k][1].wait_recv()
            near[k, 1, lo] = chip(k, left, lo).astype(BF16)
            near[k, 1, hi] = (chip(k, left, hi) + a_recv[k, 1].astype(F32)).astype(BF16)
            b_moves[k] = (
                go(near.at[k, 0], b_recv.at[k, 0], b_send.at[k, 0], b_rsem.at[k, 0], at(z, right, c)),
                go(near.at[k, 1], b_recv.at[k, 1], b_send.at[k, 1], b_rsem.at[k, 1], at(z, left, c)),
            )
        if t > 1:
            k = t - 2
            for one in b_moves[k]:
                one.wait_recv()
            summed = (
                chip(k, y, whole) + b_recv[k, 0].astype(F32) + b_recv[k, 1].astype(F32)
            )
            if order[k]:
                mine[k] = summed.astype(BF16)
                z_moves[k] = go(
                    mine.at[k], z_in.at[k], z_send.at[k], z_rsem.at[k],
                    at((z + order[k]) % NZ, y, c),
                )
            else:
                final = summed
    for k in range(NZ - 1):
        z_moves[k].wait_recv()
        final = final + z_in[k].astype(F32)
    episodes = final.shape[1]
    eye = lax.broadcasted_iota(jnp.int32, (episodes, episodes), 0) == lax.broadcasted_iota(
        jnp.int32, (episodes, episodes), 1
    )
    for i in range(final.shape[0]):
        price_grad[i] = lax.dot_general(
            final[i].astype(BF16), io[i], (((1,), (1,)), ((), ())), preferred_element_type=F32
        )
        column = jnp.sum(final[i] * share[i : i + 1, :], axis=1, keepdims=True)
        wage_grad[i : i + 1, :] = jnp.sum(
            jnp.where(eye, column, 0.0), axis=0, keepdims=True
        )
    for one in tau_moves:
        one.wait_recv()
    tau_grad[...] = (x_in[0] + x_in[1]) + (x_in[2] + x_in[3])
    for one in sends:
        one.wait_send()


def shards(
    log_prices,
    log_wages,
    labor_share,
    io_coeffs,
    pair_blocks,
    log_tau,
    elasticity,
    partners,
    list_lengths,
    price_cotangent,
):
    own, episodes, sectors = log_prices.shape
    slots = pair_blocks.shape[1]
    block = (own, episodes, sectors)
    total = NZ * NY * NC * own
    rows = pl.pallas_call(
        gather_kernel,
        out_shape=jax.ShapeDtypeStruct((NZ, NY, NC) + block, BF16),
        in_specs=[VMEM] * 4,
        out_specs=VMEM,
        scratch_shapes=[
            DMA((NZ,)), DMA((NZ,)), DMA((NZ, 2)), DMA((NZ, 2)),
            DMA((NZ, 2)), DMA((NZ, 2)), DMA((NZ,)), DMA((NZ,)),
        ],
        compiler_params=pltpu.CompilerParams(collective_id=0, has_side_effects=True),
        name="gather_costs",
    )(log_prices, log_wages, labor_share, io_coeffs)

    chunks = held_chunks(slots)
    new_prices, tau_part, pushed = pl.pallas_call(
        slots_kernel,
        out_shape=(
            jax.ShapeDtypeStruct(block, BF16),
            jax.ShapeDtypeStruct((own, slots, sectors), F32),
            jax.ShapeDtypeStruct((total, episodes, sectors), BF16),
        ),
        in_specs=[VMEM, ANY, VMEM, VMEM, ANY, ANY, VMEM],
        out_specs=(VMEM, VMEM, VMEM),
        scratch_shapes=[
            pltpu.VMEM((slots, episodes, sectors), F32),
            pltpu.VMEM((own, slots, sectors, sectors), BF16),
            pltpu.SMEM((8, slots), jnp.int32),
            pltpu.SMEM((total,), jnp.int32),
            pltpu.VMEM((slots, episodes, sectors), BF16),
            DMA((own * chunks,)),
            DMA((2,)),
        ],
        compiler_params=pltpu.CompilerParams(vmem_limit_bytes=40 << 20),
        name="slots",
    )(
        rows.reshape(total, episodes, sectors),
        pair_blocks,
        log_tau,
        elasticity.reshape(1, sectors),
        partners,
        list_lengths,
        price_cotangent,
    )

    half = (own // 2, episodes, sectors)
    price_grad, wage_grad, tau_grad = pl.pallas_call(
        scatter_kernel,
        out_shape=(
            jax.ShapeDtypeStruct(block, F32),
            jax.ShapeDtypeStruct((own, episodes), F32),
            jax.ShapeDtypeStruct((own, slots, sectors), F32),
        ),
        in_specs=[VMEM] * 4,
        out_specs=(VMEM,) * 3,
        scratch_shapes=[
            pltpu.VMEM((NZ, NY) + block, BF16),
            pltpu.VMEM((NZ,) + block, BF16),
            pltpu.VMEM((NZ, 2) + block, BF16),
            pltpu.VMEM((NZ,) + block, BF16),
            pltpu.VMEM((NZ, 2) + half, BF16),
            pltpu.VMEM((NZ, 2) + block, BF16),
            pltpu.VMEM((NZ,) + block, BF16),
            pltpu.VMEM((4, own, slots, sectors), F32),
            DMA((NZ,)), DMA((NZ,)), DMA((NZ, 2)), DMA((NZ, 2)), DMA((NZ, 2)), DMA((NZ, 2)),
            DMA((NZ,)), DMA((NZ,)), DMA((4,)), DMA((4,)),
        ],
        compiler_params=pltpu.CompilerParams(collective_id=1, has_side_effects=True),
        name="scatter_costs",
    )(pushed.reshape((NZ, NY, NC) + block), tau_part, labor_share, io_coeffs)
    return (new_prices, price_grad, wage_grad, tau_grad)


def solution(mesh):
    return jax.shard_map(
        shards,
        mesh=mesh,
        in_specs=(
            P("reg", "ep", None),
            P("reg", "ep"),
            P("reg", None),
            P("reg", None, None),
            P("reg", None, None, None),
            P("reg", None, None),
            P(),
            P(),
            P(),
            P("reg", "ep", None),
        ),
        out_specs=(
            P("reg", "ep", None),
            P("reg", "ep", None),
            P("reg", "ep"),
            P("reg", None, None),
        ),
        check_vma=False,
    )
```

time: 370 us -> 90.2 us (0.24)
  waiting for transfers between devices: 315 us -> 0 us
  Pallas kernels: 0 us -> 80.4 us
  matrix products: 25 us -> 0 us
  between operations: 14.5 us -> 0.74 us
    unnamed x4 -> x0, waiting for transfers between devices: 191 us -> none
    pallas_call x0 -> x3, Pallas kernels: none -> 80.4 us  [the longest x1 36.2 us: shards(): pl.pallas_call(gather_kernel, out_shape=jax.ShapeDtypeStruct((NZ, NY, NC)...]
    all_gather x1 -> x0, waiting for transfers between devices: 78.3 us -> none  [shards(): shard_rows = lax.all_gather(unit_cost, 'reg', axis=0, tiled=True)]
    psum x1 -> x0, waiting for transfers between devices: 45.7 us -> none  [shards(): tau_grad = lax.psum(jnp.sum(adjoint, axis=2), 'ep')]
    dot_general x6 -> x0, matrix products: 25 us -> none  [the longest x1 11.2 us: shards(): jnp.einsum('rsej,rskj->rsek', adjoint.astype(jnp.bfloat16), pair_blocks,...]
  transfers between devices with their start and end apart: 3 -> 0, of which waited for: 3 -> 0; matrix products, arithmetic and copies ran while one was open for 2% -> 0% of each run, Pallas kernels for 0% -> 0%
where the time goes in v1:
time: 90.2 us; the launch traced here: 89.9 us
  Pallas kernels  80.4 us (89%)
  local copies, waits for them, and re-layouts  8.8 us (10%)
    pallas_call x1, Pallas kernels, shards(): pl.pallas_call(gather_kernel, out_shape=jax.ShapeDtypeStruct((NZ, NY, NC)...  36.2 us
    pallas_call x1, Pallas kernels, shards(): pl.pallas_call(scatter_kernel, out_shape=(jax.ShapeDtypeStruct(block, F32...  33.1 us
    pallas_call x1, Pallas kernels, shards(): pl.pallas_call(slots_kernel, out_shape=(jax.ShapeDtypeStruct(block, BF16)...  11.1 us
    unnamed x18, local copies, waits for them, and re-layouts  8.8 us

profile of v1, /device:TPU:8, one launch (start us, length us, event | category | flops | bytes accessed | tf_op | source)
XLA Modules:
  0.0 89.9 jit_solution(3600575019341274716)
XLA Ops:
  0.6 0.0 copy-start.4
  0.6 0.0 copy-start.6
  0.7 0.0 copy-start.5
  0.7 0.0 copy-start.2
  0.7 0.9 %copy.14.partners = s32[256,32]{1,0:T(8,128)S(1)} copy(s32[256,32]{0,1:T(8,128)} %param.17) | data formatting | bytes 65536 | tf_op args[7]
  1.6 36.2 %gather_costs.1 = bf16[8,4,2,4,16,256]{5,4,3,2,1,0:T(8,128)(2,1)} custom-call(bf16[4,16,256]{2,1,0:T(8,128)(2,1)} %prices.1, f32[4,16]{1,0:T(4,128)} %wages.1, f32[4,256]{1,0:T(4,128)} %share.3, bf16[4,256,256]{2,1,0:T(8,128)(2,1)} %io.3), custom_call_target="tpu_custom_call" | custom-call | tf_op jit(solution)/shard_map/gather_costs/pallas_call | solution.py:297
  37.8 0.0 copy-done.4
  37.8 0.0 copy-done.6
  37.8 0.0 copy-done.5
  37.8 0.0 copy-done.2
  37.8 0.0 copy-start
  37.8 1.6 %copy-done = bf16[8,4,2,4,16,256]{5,4,3,2,1,0:T(8,128)(2,1)S(1)} copy-done((bf16[8,4,2,4,16,256]{5,4,3,2,1,0:T(8,128)(2,1)S(1)}, bf16[8,4,2,4,16,256]{5,4,3,2,1,0:T(8,128)(2,1)}, u32[]{:S(2)}) %copy-start) | copy-done | bytes 2097176
  39.4 11.1 %slots.1 = (bf16[4,16,256]{2,1,0:T(8,128)(2,1)}, f32[4,32,256]{2,1,0:T(8,128)S(1)}, bf16[256,16,256]{2,1,0:T(8,128)(2,1)S(1)}) custom-call(bf16[256,16,256]{2,1,0:T(8,128)(2,1)S(1)} %bitcast.3, bf16[4,32,256,256]{3,2,1,0:T(8,128)(2,1)} %blocks.1, f32[4,32,256]{2,1,0:T(8,128)S(1)} %copy-done.2, f32[1,256]{1,0:T(1,128)S(1)} %bitcast.5, ...), custom_call_target="tpu_custom_call" | custom-call | tf_op jit(solution)/shard_map/slots/pallas_call | solution.py:311
  50.5 0.0 copy-start.1
  50.5 1.3 %copy-done.1 = bf16[256,16,256]{2,1,0:T(8,128)(2,1)} copy-done((bf16[256,16,256]{2,1,0:T(8,128)(2,1)}, bf16[256,16,256]{2,1,0:T(8,128)(2,1)S(1)}, u32[]{:S(2)}) %copy-start.1) | copy-done | bytes 2097176
  51.8 0.0 copy-start.3
  51.8 0.7 copy-done.3
  52.5 33.1 %scatter_costs.1 = (f32[4,16,256]{2,1,0:T(8,128)}, f32[4,16]{1,0:T(4,128)}, f32[4,32,256]{2,1,0:T(8,128)}) custom-call(bf16[8,4,2,4,16,256]{5,4,3,2,1,0:T(8,128)(2,1)} %bitcast.4, f32[4,32,256]{2,1,0:T(8,128)} %copy-done.3, f32[4,256]{1,0:T(4,128)} %share.3, bf16[4,256,256]{2,1,0:T(8,128)(2,1)} %io.3), custom_call_target="tpu_custom_call" | custom-call | tf_op jit(solution)/shard_map/scatter_costs/pallas_call | solution.py:342
  85.6 1.5 %copy.18 = f32[4,16,256]{2,1,0:T(8,128)} copy(f32[4,16,256]{2,1,0:T(8,128)} %get-tuple-element.21) | data formatting | bytes 131072
  87.1 1.3 %copy.19 = f32[4,16]{1,0:T(4,128)} copy(f32[4,16]{1,0:T(4,128)} %get-tuple-element.22) | data formatting | bytes 512
  88.3 1.6 %copy.20 = f32[4,32,256]{2,1,0:T(8,128)} copy(f32[4,32,256]{2,1,0:T(8,128)} %get-tuple-element.23) | data formatting | bytes 262144
Async XLA Ops:
  0.6 37.1 %copy-start.4 = (f32[4,16,256]{2,1,0:T(8,128)S(1)}, f32[4,16,256]{2,1,0:T(8,128)}, u32[]{:S(2)}) copy-start(f32[4,16,256]{2,1,0:T(8,128)} %cotangent.1) | copy-start | bytes 196612
  0.6 37.1 %copy-start.6 = (s32[256]{0:T(256)S(1)}, s32[256]{0:T(256)}, u32[]{:S(2)}) copy-start(s32[256]{0:T(256)} %lengths.1) | copy-start | bytes 3076
  0.7 37.1 %copy-start.5 = (f32[256]{0:T(256)S(1)}, f32[256]{0:T(256)}, u32[]{:S(2)}) copy-start(f32[256]{0:T(256)} %param.16) | copy-start | bytes 3076
  0.7 37.1 %copy-start.2 = (f32[4,32,256]{2,1,0:T(8,128)S(1)}, f32[4,32,256]{2,1,0:T(8,128)}, u32[]{:S(2)}) copy-start(f32[4,32,256]{2,1,0:T(8,128)} %tau.1) | copy-start | bytes 393220
  37.8 1.6 %copy-start = (bf16[8,4,2,4,16,256]{5,4,3,2,1,0:T(8,128)(2,1)S(1)}, bf16[8,4,2,4,16,256]{5,4,3,2,1,0:T(8,128)(2,1)}, u32[]{:S(2)}) copy-start(bf16[8,4,2,4,16,256]{5,4,3,2,1,0:T(8,128)(2,1)} %gather_costs.1) | copy-start | bytes 6291460
  50.5 1.3 %copy-start.1 = (bf16[256,16,256]{2,1,0:T(8,128)(2,1)}, bf16[256,16,256]{2,1,0:T(8,128)(2,1)S(1)}, u32[]{:S(2)}) copy-start(bf16[256,16,256]{2,1,0:T(8,128)(2,1)S(1)} %get-tuple-element.11) | copy-start | bytes 6291460
  51.8 0.7 copy-start.3

commit v2 on v0

v2 whole, which is shorter than its diff:
```python
import jax
import jax.numpy as jnp
from jax import lax
from jax.experimental import pallas as pl
from jax.experimental.pallas import tpu as pltpu
from jax.sharding import PartitionSpec as P

NZ, NY, NC = 8, 4, 2
NEAR_FIRST = (1, 7, 2, 6, 3, 5, 4)
FAR_FIRST = (4, 5, 3, 6, 2, 7, 1, 0)
CHUNKS = 4
F32 = jnp.float32
BF16 = jnp.bfloat16
I32 = jnp.int32
MESH = pl.DeviceIdType.MESH
VMEM = pl.BlockSpec(memory_space=pltpu.VMEM)
ANY = pl.BlockSpec(memory_space=pl.ANY)
DMA = pltpu.SemaphoreType.DMA


def at(z, y, c):
    return {"reg": (z * NY + y) * NC + c}


def iota(shape, axis):
    return lax.broadcasted_iota(I32, shape, axis)


def fused_kernel(
    prices_in, wages_in, share_in, io_in, blocks, tau_in, slope_in, partners_in, lengths_in, cot_in,
    prices_out, price_grad, wage_grad, tau_sum,
    prices, wages, share, io, tau, elasticity, partners, lengths, cot, held, in_sem, b_sem,
    table, lookup, t_sem,
    rows, weights, pushed, tau_part,
    outgo, own, from_core, far, near, mine, a_in, b_in, z_in, x_in, cost,
    gz_s, gz_r, gy_s, gy_r, gh_s, gh_r, gc_s, gc_r,
    c_s, c_r, a_s, a_r, b_s, b_r, z_s, z_r, x_s, x_r,
):
    me = lax.axis_index("reg")
    z, y, c = me // (NY * NC), (me // NC) % NY, me % NC
    here, size = lax.axis_index("ep"), lax.axis_size("ep")
    right, left, across = (y + 1) % NY, (y + NY - 1) % NY, (y + 2) % NY
    regions, slots = blocks.shape[0], blocks.shape[1]
    episodes, sectors = cot.shape[1], cot.shape[2]
    total = rows.shape[0]
    half = regions // 2
    group = NY * regions

    barrier = pltpu.get_barrier_semaphore()
    peers = [at((z + d) % NZ, y, c) for d in range(1, NZ)]
    peers += [at(z, right, c), at(z, left, c), at(z, y, 1 - c)]
    peers += [{"ep": (here + d) % size} for d in range(1, size)]
    for peer in peers:
        pl.semaphore_signal(barrier, inc=1, device_id=peer, device_id_type=MESH)

    loads = [
        pltpu.make_async_copy(src, dst, in_sem.at[i])
        for i, (src, dst) in enumerate(
            (
                (io_in, io), (prices_in, prices), (wages_in, wages), (share_in, share),
                (partners_in, partners), (lengths_in, lengths), (slope_in, elasticity),
                (tau_in, tau), (cot_in, cot),
            )
        )
    ]
    for one in loads:
        one.start()
    step = slots // CHUNKS

    def block_load(n, q):
        part = pl.ds(q * step, step)
        return pltpu.make_async_copy(
            blocks.at[n, part], held.at[n, part], b_sem.at[n * CHUNKS + q]
        )

    for n in range(regions):
        for q in range(CHUNKS):
            block_load(n, q).start()

    sends = []

    def copy(src, dst, ssem, rsem, dev):
        return pltpu.make_async_remote_copy(
            src_ref=src, dst_ref=dst, send_sem=ssem, recv_sem=rsem,
            device_id=dev, device_id_type=MESH,
        )

    def go(*args):
        one = copy(*args)
        one.start()
        sends.append(one)
        return one

    def first(zz, cc, yy):
        return ((zz * NC + cc) * NY + yy) * regions

    for one in loads[:4]:
        one.wait()
    eye = iota((episodes, episodes), 0) == iota((episodes, episodes), 1)
    for i in range(regions):
        column = jnp.sum(jnp.where(eye, wages[i : i + 1, :], 0.0), axis=1, keepdims=True)
        unit = column * share[i : i + 1, :] + jnp.dot(
            prices[i], io[i], preferred_element_type=F32
        )
        rows[first(z, c, y) + i] = unit.astype(BF16)
    pl.semaphore_wait(barrier, len(peers))

    def block(zz, yy, off=0, count=regions):
        return rows.at[pl.ds(first(zz, c, yy) + off, count)]

    def shared(zz, cc):
        return rows.at[pl.ds(first(zz, cc, 0), group)]

    def push(ref, ssem, rsem, dev):
        go(ref, ref, ssem, rsem, dev)

    def land(ref, ssem, rsem):
        copy(ref, ref, ssem, rsem, at(z, y, c)).wait_recv()

    def both_ways(k, ref):
        push(ref, gy_s.at[k, 0], gy_r.at[k, 0], at(z, right, c))
        push(ref, gy_s.at[k, 1], gy_r.at[k, 1], at(z, left, c))

    mine_rows = block(z, y)
    for d in NEAR_FIRST[:2]:
        push(mine_rows, gz_s.at[d], gz_r.at[d], at((z + d) % NZ, y, c))
    both_ways(0, mine_rows)
    for d in NEAR_FIRST[2:]:
        push(mine_rows, gz_s.at[d], gz_r.at[d], at((z + d) % NZ, y, c))

    for one in loads[4:6]:
        one.wait()
    lanes = iota((slots, total), 1)
    rank = iota((slots, total), 0)
    lane_eye = rank == lanes
    for n in range(regions):
        pick = lanes == me * regions + n
        named = jnp.sum(jnp.where(pick, partners[...], 0), axis=1, keepdims=True)
        length = jnp.sum(jnp.where(pick[:1], lengths[...], 0), axis=1, keepdims=True)
        zz, yy, cc = named // (NY * NC * regions), (named // (NC * regions)) % NY, (named // regions) % NC
        named = first(zz, cc, yy) + named % regions
        live = rank < length
        where = jnp.min(
            jnp.where((named == lanes) & live, rank + n * slots, regions * slots),
            axis=0, keepdims=True,
        )
        table[n : n + 1, :] = where
        whom = jnp.sum(jnp.where(lane_eye, named, 0), axis=0, keepdims=True)
        table[regions + n : regions + n + 1, :] = jnp.where(lanes[:1] == slots, length, whom)
    pushed[regions * slots] = jnp.zeros((episodes, sectors), BF16)

    for d in NEAR_FIRST:
        ref = block((z + NZ - d) % NZ, y)
        land(ref, gz_s.at[d], gz_r.at[d])
        both_ways(d, ref)
    to_lookup = pltpu.make_async_copy(table, lookup, t_sem.at[0])
    to_lookup.start()
    for k in (0,) + NEAR_FIRST:
        zz = (z + NZ - k) % NZ
        land(block(zz, left), gy_s.at[k, 0], gy_r.at[k, 0])
        push(block(zz, left, 0, half), gh_s.at[k, 0], gh_r.at[k, 0], at(z, right, c))
        land(block(zz, right), gy_s.at[k, 1], gy_r.at[k, 1])
        push(block(zz, right, half, half), gh_s.at[k, 1], gh_r.at[k, 1], at(z, left, c))
    for k in (0,) + NEAR_FIRST:
        zz = (z + NZ - k) % NZ
        land(block(zz, across, 0, half), gh_s.at[k, 0], gh_r.at[k, 0])
        land(block(zz, across, half, half), gh_s.at[k, 1], gh_r.at[k, 1])
        push(shared(zz, c), gc_s.at[k], gc_r.at[k], at(z, y, 1 - c))
    to_lookup.wait()
    for one in loads[6:]:
        one.wait()
    for k in (0,) + NEAR_FIRST:
        land(shared((z + NZ - k) % NZ, 1 - c), gc_s.at[k], gc_r.at[k])

    def importer(n, carry):
        slope = -elasticity[...]
        length = lookup[regions + n, slots]
        top = jnp.full((episodes, sectors), -jnp.inf, F32)
        for q in range(CHUNKS):
            block_load(n, q).wait()
            for s in range(q * step, (q + 1) * step):
                landed = tau[n, s : s + 1, :] + jnp.dot(
                    rows[lookup[regions + n, s]], held[n, s], preferred_element_type=F32
                )
                score = jnp.where(s < length, slope * landed, -jnp.inf)
                weights[s] = score
                top = jnp.maximum(top, score)
        summed = jnp.zeros((episodes, sectors), F32)
        for s in range(slots):
            one = jnp.exp(weights[s] - top)
            weights[s] = one
            summed = summed + one
        prices_out[n] = (-(top + jnp.log(summed)) / elasticity[...]).astype(BF16)
        scale = cot[n] / summed
        for s in range(slots):
            one = weights[s] * scale
            tau_part[n, s : s + 1, :] = jnp.sum(one, axis=0, keepdims=True)
            pushed[n * slots + s] = lax.dot_general(
                one.astype(BF16), held[n, s], (((1,), (1,)), ((), ())),
                preferred_element_type=F32,
            ).astype(BF16)
        return carry

    lax.fori_loop(0, regions, importer, 0)

    def fill(dst, k, cc):
        base = first((z + FAR_FIRST[k]) % NZ, cc, 0)

        def some(r, carry):
            for i in range(regions):
                at_row = r * regions + i
                value = pushed[lookup[0, base + at_row]].astype(F32)
                for n in range(1, regions):
                    value = value + pushed[lookup[n, base + at_row]].astype(F32)
                dst[k, at_row] = value.astype(BF16)
            return carry

        lax.fori_loop(0, NY, some, 0)

    core_moves = []
    for k in range(NZ):
        fill(outgo, k, 1 - c)
        core_moves.append(
            go(outgo.at[k], from_core.at[k], c_s.at[k], c_r.at[k], at(z, y, 1 - c))
        )
    tau_moves = [
        go(tau_part, x_in.at[here], x_s.at[d], x_r.at[d], {"ep": (here + d) % size})
        for d in range(1, size)
    ]
    x_in[here] = tau_part[...]
    for k in range(NZ):
        fill(own, k, c)

    def chip(k, yy, off, count):
        part = pl.ds(yy * regions + off, count)
        return own[k, part].astype(F32) + from_core[k, part].astype(F32)

    a_moves, b_moves, z_moves = [], [], []
    for k in range(NZ):
        core_moves[k].wait_recv()
        far[k] = chip(k, across, 0, regions).astype(BF16)
        a_moves.append((
            go(far.at[k, :half], a_in.at[k, 0], a_s.at[k, 0], a_r.at[k, 0], at(z, right, c)),
            go(far.at[k, half:], a_in.at[k, 1], a_s.at[k, 1], a_r.at[k, 1], at(z, left, c)),
        ))
    for k in range(NZ):
        a_moves[k][0].wait_recv()
        near[k, 0, :half] = (chip(k, right, 0, half) + a_in[k, 0].astype(F32)).astype(BF16)
        near[k, 0, half:] = chip(k, right, half, half).astype(BF16)
        a_moves[k][1].wait_recv()
        near[k, 1, :half] = chip(k, left, 0, half).astype(BF16)
        near[k, 1, half:] = (chip(k, left, half, half) + a_in[k, 1].astype(F32)).astype(BF16)
        b_moves.append((
            go(near.at[k, 0], b_in.at[k, 0], b_s.at[k, 0], b_r.at[k, 0], at(z, right, c)),
            go(near.at[k, 1], b_in.at[k, 1], b_s.at[k, 1], b_r.at[k, 1], at(z, left, c)),
        ))
    for k in range(NZ):
        for one in b_moves[k]:
            one.wait_recv()
        summed = chip(k, y, 0, regions) + b_in[k, 0].astype(F32) + b_in[k, 1].astype(F32)
        d = FAR_FIRST[k]
        if d:
            mine[k] = summed.astype(BF16)
            z_moves.append(
                go(mine.at[k], z_in.at[k], z_s.at[k], z_r.at[k], at((z + d) % NZ, y, c))
            )
        else:
            cost[...] = summed
    for one in tau_moves:
        one.wait_recv()
    tau_sum[...] = (x_in[0] + x_in[1]) + (x_in[2] + x_in[3])
    for k in range(NZ - 1):
        z_moves[k].wait_recv()
    final = cost[...]
    for k in range(NZ - 1):
        final = final + z_in[k].astype(F32)
    for i in range(regions):
        price_grad[i] = lax.dot_general(
            final[i].astype(BF16), io[i], (((1,), (1,)), ((), ())), preferred_element_type=F32
        )
        column = jnp.sum(final[i] * share[i : i + 1, :], axis=1, keepdims=True)
        wage_grad[i : i + 1, :] = jnp.sum(jnp.where(eye, column, 0.0), axis=0, keepdims=True)
    for one in sends:
        one.wait_send()


def finish_kernel(*refs):
    count = (len(refs) - 2) // 3
    source, result, held = refs[:count], refs[count : 2 * count], refs[2 * count : 3 * count]
    in_sem, out_sem = refs[-2:]
    ins = [pltpu.make_async_copy(source[i], held[i], in_sem.at[i]) for i in range(count)]
    outs = [pltpu.make_async_copy(held[i], result[i], out_sem.at[i]) for i in range(count)]
    for one in ins:
        one.start()
    for one, then in zip(ins, outs):
        one.wait()
        then.start()
    for one in outs:
        one.wait()


def shards(
    log_prices,
    log_wages,
    labor_share,
    io_coeffs,
    pair_blocks,
    log_tau,
    elasticity,
    partners,
    list_lengths,
    price_cotangent,
):
    own, episodes, sectors = log_prices.shape
    slots = pair_blocks.shape[1]
    block = (own, episodes, sectors)
    half = (own // 2, episodes, sectors)
    group = (NY * own, episodes, sectors)
    total = NZ * NY * NC * own
    tau_shape = (own, slots, sectors)
    vm = pltpu.VMEM
    outs = (
        jax.ShapeDtypeStruct(block, BF16),
        jax.ShapeDtypeStruct(block, F32),
        jax.ShapeDtypeStruct((own, episodes), F32),
        jax.ShapeDtypeStruct(tau_shape, F32),
    )
    results = pl.pallas_call(
        fused_kernel,
        out_shape=outs,
        in_specs=[ANY] * 10,
        out_specs=(VMEM,) * 4,
        scratch_shapes=[
            vm(block, BF16), vm((own, episodes), F32), vm((own, sectors), F32),
            vm((own, sectors, sectors), BF16), vm(tau_shape, F32), vm((1, sectors), F32),
            vm((slots, total), I32), vm((1, total), I32), vm(block, F32),
            vm((own, slots, sectors, sectors), BF16), DMA((9,)), DMA((own * CHUNKS,)),
            vm((2 * own, total), I32), pltpu.SMEM((2 * own, total), I32), DMA((1,)),
            vm((total, episodes, sectors), BF16), vm((slots, episodes, sectors), F32),
            vm((own * slots + 1, episodes, sectors), BF16), vm(tau_shape, F32),
            vm((NZ,) + group, BF16), vm((NZ,) + group, BF16), vm((NZ,) + group, BF16),
            vm((NZ,) + block, BF16), vm((NZ, 2) + block, BF16), vm((NZ,) + block, BF16),
            vm((NZ, 2) + half, BF16), vm((NZ, 2) + block, BF16), vm((NZ,) + block, BF16),
            vm((4,) + tau_shape, F32), vm(block, F32),
            DMA((NZ,)), DMA((NZ,)), DMA((NZ, 2)), DMA((NZ, 2)), DMA((NZ, 2)), DMA((NZ, 2)),
            DMA((NZ,)), DMA((NZ,)),
            DMA((NZ,)), DMA((NZ,)), DMA((NZ, 2)), DMA((NZ, 2)), DMA((NZ, 2)), DMA((NZ, 2)),
            DMA((NZ,)), DMA((NZ,)), DMA((4,)), DMA((4,)),
        ],
        compiler_params=pltpu.CompilerParams(
            collective_id=0, has_side_effects=True, vmem_limit_bytes=60 * 1024 * 1024
        ),
        name="iteration",
    )(
        log_prices, log_wages, labor_share, io_coeffs, pair_blocks, log_tau,
        elasticity.reshape(1, sectors), partners.T, list_lengths.reshape(1, total),
        price_cotangent,
    )
    return pl.pallas_call(
        finish_kernel,
        out_shape=outs,
        in_specs=[ANY] * 4,
        out_specs=(ANY,) * 4,
        scratch_shapes=[vm(one.shape, one.dtype) for one in outs] + [DMA((4,)), DMA((4,))],
        compiler_params=pltpu.CompilerParams(vmem_limit_bytes=60 * 1024 * 1024),
        name="finish",
    )(*results)


def solution(mesh):
    return jax.shard_map(
        shards,
        mesh=mesh,
        in_specs=(
            P("reg", "ep", None),
            P("reg", "ep"),
            P("reg", None),
            P("reg", None, None),
            P("reg", None, None, None),
            P("reg", None, None),
            P(),
            P(),
            P(),
            P("reg", "ep", None),
        ),
        out_specs=(
            P("reg", "ep", None),
            P("reg", "ep", None),
            P("reg", "ep"),
            P("reg", None, None),
        ),
        check_vma=False,
    )
```

time: 370 us -> 59.8 us (0.16)
  the two profiles are of different devices: /device:TPU:8 before, /device:TPU:1 now
where the time goes in v2:
time: 59.8 us; the launch traced here: 59.7 us
  Pallas kernels  59.1 us (99%)
  between operations  0.64 us (1%)
    pallas_call x1, Pallas kernels, shards(): pl.pallas_call(fused_kernel, out_shape=outs, in_specs=[ANY] * 10, out_spe...  57.4 us
    pallas_call x1, Pallas kernels, shards(): pl.pallas_call(finish_kernel, out_shape=outs, in_specs=[ANY] * 4, out_spe...  1.69 us

profile of v2, /device:TPU:1, one launch (start us, length us, event | category | flops | bytes accessed | tf_op | source)
XLA Modules:
  0.0 59.7 jit_solution(8724957210863576573)
XLA Ops:
  0.6 57.4 %iteration.1 = (bf16[4,16,256]{2,1,0:T(8,128)(2,1)}, f32[4,16,256]{2,1,0:T(8,128)}, f32[4,16]{1,0:T(4,128)}, f32[4,32,256]{2,1,0:T(8,128)}) custom-call(bf16[4,16,256]{2,1,0:T(8,128)(2,1)} %prices_in.1, f32[4,16]{1,0:T(4,128)} %wages_in.1, f32[4,256]{1,0:T(4,128)} %share_in.1, bf16[4,256,256]{2,1,0:T(8,128)(2,1)} %io_in.1, bf16[4,32,256,256]{3,2,1,0:T(8,128)(2,1)} %blocks.1, ...), custom_call_target="tpu_custom_call" | custom-call | tf_op jit(solution)/shard_map/iteration/pallas_call | solution.py:328
  58.1 1.7 %finish.1 = (bf16[4,16,256]{2,1,0:T(8,128)(2,1)}, f32[4,16,256]{2,1,0:T(8,128)}, f32[4,16]{1,0:T(4,128)}, f32[4,32,256]{2,1,0:T(8,128)}) custom-call(bf16[4,16,256]{2,1,0:T(8,128)(2,1)} %get-tuple-element.8.refs_0_, f32[4,16,256]{2,1,0:T(8,128)} %get-tuple-element.9.refs_1_, f32[4,16]{1,0:T(4,128)} %get-tuple-element.10.refs_2_, ...), custom_call_target="tpu_custom_call" | custom-call | tf_op jit(solution)/shard_map/finish/pallas_call | solution.py:359

commit v3 on v2

--- a/solution.py
+++ b/solution.py
@@ -6,8 +6,9 @@
 from jax.sharding import PartitionSpec as P
 
 NZ, NY, NC = 8, 4, 2
-NEAR_FIRST = (1, 7, 2, 6, 3, 5, 4)
-FAR_FIRST = (4, 5, 3, 6, 2, 7, 1, 0)
+FAR = (2, 6, 3, 5, 4)
+BESIDE = (1, 7)
+ORDER = (4, 5, 3, 1, 7, 6, 2, 0)
 CHUNKS = 4
 F32 = jnp.float32
 BF16 = jnp.bfloat16
@@ -32,9 +33,9 @@
     prices, wages, share, io, tau, elasticity, partners, lengths, cot, held, in_sem, b_sem,
     table, lookup, t_sem,
     rows, weights, pushed, tau_part,
-    outgo, own, from_core, far, near, mine, a_in, b_in, z_in, x_in, cost,
-    gz_s, gz_r, gy_s, gy_r, gh_s, gh_r, gc_s, gc_r,
-    c_s, c_r, a_s, a_r, b_s, b_r, z_s, z_r, x_s, x_r,
+    outgo, own, from_core, near, y_in, slab, v_in, mine, z_in, x_in,
+    gz_s, gz_r, gy_s, gy_r, gv_s, gv_r, gc_s, gc_r,
+    c_s, c_r, y_s, y_r, v_s, v_r, z_s, z_r, x_s, x_r,
 ):
     me = lax.axis_index("reg")
     z, y, c = me // (NY * NC), (me // NC) % NY, me % NC
@@ -43,12 +44,11 @@
     regions, slots = blocks.shape[0], blocks.shape[1]
     episodes, sectors = cot.shape[1], cot.shape[2]
     total = rows.shape[0]
-    half = regions // 2
     group = NY * regions
 
     barrier = pltpu.get_barrier_semaphore()
     peers = [at((z + d) % NZ, y, c) for d in range(1, NZ)]
-    peers += [at(z, right, c), at(z, left, c), at(z, y, 1 - c)]
+    peers += [at(z, right, c), at(z, left, c), at(z, across, c), at(z, y, 1 - c)]
     peers += [{"ep": (here + d) % size} for d in range(1, size)]
     for peer in peers:
         pl.semaphore_signal(barrier, inc=1, device_id=peer, device_id_type=MESH)
@@ -73,10 +73,6 @@
             blocks.at[n, part], held.at[n, part], b_sem.at[n * CHUNKS + q]
         )
 
-    for n in range(regions):
-        for q in range(CHUNKS):
-            block_load(n, q).start()
-
     sends = []
 
     def copy(src, dst, ssem, rsem, dev):
@@ -105,8 +101,8 @@
         rows[first(z, c, y) + i] = unit.astype(BF16)
     pl.semaphore_wait(barrier, len(peers))
 
-    def block(zz, yy, off=0, count=regions):
-        return rows.at[pl.ds(first(zz, c, yy) + off, count)]
+    def block(zz, yy):
+        return rows.at[pl.ds(first(zz, c, yy), regions)]
 
     def shared(zz, cc):
         return rows.at[pl.ds(first(zz, cc, 0), group)]
@@ -117,16 +113,29 @@
     def land(ref, ssem, rsem):
         copy(ref, ref, ssem, rsem, at(z, y, c)).wait_recv()
 
-    def both_ways(k, ref):
-        push(ref, gy_s.at[k, 0], gy_r.at[k, 0], at(z, right, c))
-        push(ref, gy_s.at[k, 1], gy_r.at[k, 1], at(z, left, c))
-
-    mine_rows = block(z, y)
-    for d in NEAR_FIRST[:2]:
-        push(mine_rows, gz_s.at[d], gz_r.at[d], at((z + d) % NZ, y, c))
-    both_ways(0, mine_rows)
-    for d in NEAR_FIRST[2:]:
-        push(mine_rows, gz_s.at[d], gz_r.at[d], at((z + d) % NZ, y, c))
+    def around(k, ref):
+        for j, yy in ((0, across), (1, right), (2, left)):
+            push(ref, gy_s.at[k, j], gy_r.at[k, j], at(z, yy, c))
+
+    def around_landed(k):
+        zz = (z + NZ - k) % NZ
+        for j, yy in ((1, left), (2, right), (0, across)):
+            land(block(zz, yy), gy_s.at[k, j], gy_r.at[k, j])
+
+    def beside(j, yy):
+        for i, d in enumerate(BESIDE):
+            push(block(z, yy), gv_s.at[i, j], gv_r.at[i, j], at((z + d) % NZ, y, c))
+
+    def to_partner(k):
+        push(shared((z + NZ - k) % NZ, c), gc_s.at[k], gc_r.at[k], at(z, y, 1 - c))
+
+    beside(0, y)
+    around(0, block(z, y))
+    for d in FAR:
+        push(block(z, y), gz_s.at[d], gz_r.at[d], at((z + d) % NZ, y, c))
+    for n in range(regions):
+        for q in range(CHUNKS):
+            block_load(n, q).start()
 
     for one in loads[4:6]:
         one.wait()
@@ -149,27 +158,33 @@
         table[regions + n : regions + n + 1, :] = jnp.where(lanes[:1] == slots, length, whom)
     pushed[regions * slots] = jnp.zeros((episodes, sectors), BF16)
 
-    for d in NEAR_FIRST:
+    to_lookup = pltpu.make_async_copy(table, lookup, t_sem.at[0])
+
+    def far_landed(d):
         ref = block((z + NZ - d) % NZ, y)
         land(ref, gz_s.at[d], gz_r.at[d])
-        both_ways(d, ref)
-    to_lookup = pltpu.make_async_copy(table, lookup, t_sem.at[0])
+        around(d, ref)
+
+    for d in FAR[:2]:
+        far_landed(d)
+    around_landed(0)
+    for j, yy in enumerate((left, right, across)):
+        beside(j + 1, yy)
+    to_partner(0)
+    for d in FAR[2:]:
+        far_landed(d)
     to_lookup.start()
-    for k in (0,) + NEAR_FIRST:
-        zz = (z + NZ - k) % NZ
-        land(block(zz, left), gy_s.at[k, 0], gy_r.at[k, 0])
-        push(block(zz, left, 0, half), gh_s.at[k, 0], gh_r.at[k, 0], at(z, right, c))
-        land(block(zz, right), gy_s.at[k, 1], gy_r.at[k, 1])
-        push(block(zz, right, half, half), gh_s.at[k, 1], gh_r.at[k, 1], at(z, left, c))
-    for k in (0,) + NEAR_FIRST:
-        zz = (z + NZ - k) % NZ
-        land(block(zz, across, 0, half), gh_s.at[k, 0], gh_r.at[k, 0])
-        land(block(zz, across, half, half), gh_s.at[k, 1], gh_r.at[k, 1])
-        push(shared(zz, c), gc_s.at[k], gc_r.at[k], at(z, y, 1 - c))
+    for i, d in enumerate(BESIDE):
+        for j, yy in enumerate((y, left, right, across)):
+            land(block((z + NZ - d) % NZ, yy), gv_s.at[i, j], gv_r.at[i, j])
+        to_partner(d)
+    for d in FAR:
+        around_landed(d)
+        to_partner(d)
     to_lookup.wait()
     for one in loads[6:]:
         one.wait()
-    for k in (0,) + NEAR_FIRST:
+    for k in (0,) + BESIDE + FAR:
         land(shared((z + NZ - k) % NZ, 1 - c), gc_s.at[k], gc_r.at[k])
 
     def importer(n, carry):
@@ -204,7 +219,7 @@
     lax.fori_loop(0, regions, importer, 0)
 
     def fill(dst, k, cc):
-        base = first((z + FAR_FIRST[k]) % NZ, cc, 0)
+        base = first((z + ORDER[k]) % NZ, cc, 0)
 
         def some(r, carry):
             for i in range(regions):
@@ -231,48 +246,70 @@
     for k in range(NZ):
         fill(own, k, c)
 
-    def chip(k, yy, off, count):
-        part = pl.ds(yy * regions + off, count)
+    def chip(k, yy):
+        part = pl.ds(yy * regions, regions)
         return own[k, part].astype(F32) + from_core[k, part].astype(F32)
 
-    a_moves, b_moves, z_moves = [], [], []
-    for k in range(NZ):
+    ways = ((0, across), (1, right), (2, left))
+    y_moves, z_moves, v_moves = {}, [], []
+
+    def send_around(k, value):
+        for j, yy in ways:
+            near[k, j] = value(yy).astype(BF16)
+        y_moves[k] = [
+            go(near.at[k, j], y_in.at[k, j], y_s.at[k, j], y_r.at[k, j], at(z, yy, c))
+            for j, yy in ways
+        ]
+
+    def came_around(k):
+        value = None
+        for j in (1, 2, 0):
+            y_moves[k][j].wait_recv()
+            term = y_in[k, j].astype(F32)
+            value = term if value is None else value + term
+        return value
+
+    for k in range(NZ - 1):
         core_moves[k].wait_recv()
-        far[k] = chip(k, across, 0, regions).astype(BF16)
-        a_moves.append((
-            go(far.at[k, :half], a_in.at[k, 0], a_s.at[k, 0], a_r.at[k, 0], at(z, right, c)),
-            go(far.at[k, half:], a_in.at[k, 1], a_s.at[k, 1], a_r.at[k, 1], at(z, left, c)),
-        ))
-    for k in range(NZ):
-        a_moves[k][0].wait_recv()
-        near[k, 0, :half] = (chip(k, right, 0, half) + a_in[k, 0].astype(F32)).astype(BF16)
-        near[k, 0, half:] = chip(k, right, half, half).astype(BF16)
-        a_moves[k][1].wait_recv()
-        near[k, 1, :half] = chip(k, left, 0, half).astype(BF16)
-        near[k, 1, half:] = (chip(k, left, half, half) + a_in[k, 1].astype(F32)).astype(BF16)
-        b_moves.append((
-            go(near.at[k, 0], b_in.at[k, 0], b_s.at[k, 0], b_r.at[k, 0], at(z, right, c)),
-            go(near.at[k, 1], b_in.at[k, 1], b_s.at[k, 1], b_r.at[k, 1], at(z, left, c)),
-        ))
-    for k in range(NZ):
-        for one in b_moves[k]:
-            one.wait_recv()
-        summed = chip(k, y, 0, regions) + b_in[k, 0].astype(F32) + b_in[k, 1].astype(F32)
-        d = FAR_FIRST[k]
-        if d:
-            mine[k] = summed.astype(BF16)
-            z_moves.append(
-                go(mine.at[k], z_in.at[k], z_s.at[k], z_r.at[k], at((z + d) % NZ, y, c))
+        d = ORDER[k]
+        if d in BESIDE:
+            i = BESIDE.index(d)
+            for r in range(NY):
+                part = pl.ds(r * regions, regions)
+                slab[i, part] = chip(k, r).astype(BF16)
+            v_moves.append(
+                go(slab.at[i], v_in.at[i], v_s.at[i], v_r.at[i], at((z + d) % NZ, y, c))
             )
         else:
-            cost[...] = summed
+            send_around(k, lambda yy: chip(k, yy))
+
+    def send_far(k):
+        mine[k] = (chip(k, y) + came_around(k)).astype(BF16)
+        z_moves.append((k, go(
+            mine.at[k], z_in.at[k], z_s.at[k], z_r.at[k], at((z + ORDER[k]) % NZ, y, c)
+        )))
+
+    last = NZ - 1
+    far = [k for k in range(last) if ORDER[k] not in BESIDE]
+    for k in far[:2]:
+        send_far(k)
+    core_moves[last].wait_recv()
+    for one in v_moves:
+        one.wait_recv()
+
+    def own_chunk(yy):
+        part = pl.ds(yy * regions, regions)
+        return chip(last, yy) + (v_in[0, part].astype(F32) + v_in[1, part].astype(F32))
+
+    send_around(last, own_chunk)
+    for k in far[2:]:
+        send_far(k)
     for one in tau_moves:
         one.wait_recv()
     tau_sum[...] = (x_in[0] + x_in[1]) + (x_in[2] + x_in[3])
-    for k in range(NZ - 1):
-        z_moves[k].wait_recv()
-    final = cost[...]
-    for k in range(NZ - 1):
+    final = own_chunk(y) + came_around(last)
+    for k, one in z_moves[::-1]:
+        one.wait_recv()
         final = final + z_in[k].astype(F32)
     for i in range(regions):
         price_grad[i] = lax.dot_general(
@@ -314,7 +351,6 @@
     own, episodes, sectors = log_prices.shape
     slots = pair_blocks.shape[1]
     block = (own, episodes, sectors)
-    half = (own // 2, episodes, sectors)
     group = (NY * own, episodes, sectors)
     total = NZ * NY * NC * own
     tau_shape = (own, slots, sectors)
@@ -339,12 +375,12 @@
             vm((total, episodes, sectors), BF16), vm((slots, episodes, sectors), F32),
             vm((own * slots + 1, episodes, sectors), BF16), vm(tau_shape, F32),
             vm((NZ,) + group, BF16), vm((NZ,) + group, BF16), vm((NZ,) + group, BF16),
-            vm((NZ,) + block, BF16), vm((NZ, 2) + block, BF16), vm((NZ,) + block, BF16),
-            vm((NZ, 2) + half, BF16), vm((NZ, 2) + block, BF16), vm((NZ,) + block, BF16),
-            vm((4,) + tau_shape, F32), vm(block, F32),
-            DMA((NZ,)), DMA((NZ,)), DMA((NZ, 2)), DMA((NZ, 2)), DMA((NZ, 2)), DMA((NZ, 2)),
+            vm((NZ, 3) + block, BF16), vm((NZ, 3) + block, BF16), vm((2,) + group, BF16),
+            vm((2,) + group, BF16), vm((NZ,) + block, BF16), vm((NZ,) + block, BF16),
+            vm((4,) + tau_shape, F32),
+            DMA((NZ,)), DMA((NZ,)), DMA((NZ, 3)), DMA((NZ, 3)), DMA((2, 4)), DMA((2, 4)),
             DMA((NZ,)), DMA((NZ,)),
-            DMA((NZ,)), DMA((NZ,)), DMA((NZ, 2)), DMA((NZ, 2)), DMA((NZ, 2)), DMA((NZ, 2)),
+            DMA((NZ,)), DMA((NZ,)), DMA((NZ, 3)), DMA((NZ, 3)), DMA((2,)), DMA((2,)),
             DMA((NZ,)), DMA((NZ,)), DMA((4,)), DMA((4,)),
         ],
         compiler_params=pltpu.CompilerParams(

time: 59.8 us -> 54.1 us (0.905)
  Pallas kernels: 59.1 us -> 53.3 us
    pallas_call x1, Pallas kernels: 57.4 us -> 51.6 us  [shards(): pl.pallas_call(fused_kernel, out_shape=outs, in_specs=[ANY] * 10, out_spe...]
where the time goes in v3:
time: 54.1 us; the launch traced here: 54 us
  Pallas kernels  53.3 us (99%)
  between operations  0.64 us (1%)
    pallas_call x1, Pallas kernels, shards(): pl.pallas_call(fused_kernel, out_shape=outs, in_specs=[ANY] * 10, out_spe...  51.6 us
    pallas_call x1, Pallas kernels, shards(): pl.pallas_call(finish_kernel, out_shape=outs, in_specs=[ANY] * 4, out_spe...  1.69 us

profile of v3, /device:TPU:1, one launch (start us, length us, event | category | flops | bytes accessed | tf_op | source)
XLA Modules:
  0.0 54.0 jit_solution(3926090275803143369)
XLA Ops:
  0.6 51.6 %iteration.1 = (bf16[4,16,256]{2,1,0:T(8,128)(2,1)}, f32[4,16,256]{2,1,0:T(8,128)}, f32[4,16]{1,0:T(4,128)}, f32[4,32,256]{2,1,0:T(8,128)}) custom-call(bf16[4,16,256]{2,1,0:T(8,128)(2,1)} %prices_in.1, f32[4,16]{1,0:T(4,128)} %wages_in.1, f32[4,256]{1,0:T(4,128)} %share_in.1, bf16[4,256,256]{2,1,0:T(8,128)(2,1)} %io_in.1, bf16[4,32,256,256]{3,2,1,0:T(8,128)(2,1)} %blocks.1, ...), custom_call_target="tpu_custom_call" | custom-call | tf_op jit(solution)/shard_map/iteration/pallas_call | solution.py:364
  52.3 1.7 %finish.1 = (bf16[4,16,256]{2,1,0:T(8,128)(2,1)}, f32[4,16,256]{2,1,0:T(8,128)}, f32[4,16]{1,0:T(4,128)}, f32[4,32,256]{2,1,0:T(8,128)}) custom-call(bf16[4,16,256]{2,1,0:T(8,128)(2,1)} %get-tuple-element.8.refs_0_, f32[4,16,256]{2,1,0:T(8,128)} %get-tuple-element.9.refs_1_, f32[4,16]{1,0:T(4,128)} %get-tuple-element.10.refs_2_, ...), custom_call_target="tpu_custom_call" | custom-call | tf_op jit(solution)/shard_map/finish/pallas_call | solution.py:395

commit v4 on v3

--- a/solution.py
+++ b/solution.py
@@ -10,6 +10,7 @@
 BESIDE = (1, 7)
 ORDER = (4, 5, 3, 1, 7, 6, 2, 0)
 CHUNKS = 4
+LOG2E, LN2 = 1.4426950408889634, 0.6931471805599453
 F32 = jnp.float32
 BF16 = jnp.bfloat16
 I32 = jnp.int32
@@ -188,7 +189,8 @@
         land(shared((z + NZ - k) % NZ, 1 - c), gc_s.at[k], gc_r.at[k])
 
     def importer(n, carry):
-        slope = -elasticity[...]
+        scale2 = elasticity[...] * LOG2E
+        slope = -scale2
         length = lookup[regions + n, slots]
         top = jnp.full((episodes, sectors), -jnp.inf, F32)
         for q in range(CHUNKS):
@@ -202,10 +204,10 @@
                 top = jnp.maximum(top, score)
         summed = jnp.zeros((episodes, sectors), F32)
         for s in range(slots):
-            one = jnp.exp(weights[s] - top)
+            one = jnp.exp2(weights[s] - top)
             weights[s] = one
             summed = summed + one
-        prices_out[n] = (-(top + jnp.log(summed)) / elasticity[...]).astype(BF16)
+        prices_out[n] = (-(top * LN2 + jnp.log(summed)) / elasticity[...]).astype(BF16)
         scale = cot[n] / summed
         for s in range(slots):
             one = weights[s] * scale
@@ -221,16 +223,11 @@
     def fill(dst, k, cc):
         base = first((z + ORDER[k]) % NZ, cc, 0)
 
-        def some(r, carry):
-            for i in range(regions):
-                at_row = r * regions + i
-                value = pushed[lookup[0, base + at_row]].astype(F32)
-                for n in range(1, regions):
-                    value = value + pushed[lookup[n, base + at_row]].astype(F32)
-                dst[k, at_row] = value.astype(BF16)
-            return carry
-
-        lax.fori_loop(0, NY, some, 0)
+        for at_row in range(group):
+            terms = [pushed[lookup[n, base + at_row]] for n in range(regions)]
+            while len(terms) > 1:
+                terms = [sum(terms[j + 1 : j + 2], terms[j]) for j in range(0, len(terms), 2)]
+            dst[k, at_row] = terms[0]
 
     core_moves = []
     for k in range(NZ):
@@ -243,9 +240,6 @@
         for d in range(1, size)
     ]
     x_in[here] = tau_part[...]
-    for k in range(NZ):
-        fill(own, k, c)
-
     def chip(k, yy):
         part = pl.ds(yy * regions, regions)
         return own[k, part].astype(F32) + from_core[k, part].astype(F32)
@@ -270,6 +264,7 @@
         return value
 
     for k in range(NZ - 1):
+        fill(own, k, c)
         core_moves[k].wait_recv()
         d = ORDER[k]
         if d in BESIDE:
@@ -293,6 +288,7 @@
     far = [k for k in range(last) if ORDER[k] not in BESIDE]
     for k in far[:2]:
         send_far(k)
+    fill(own, last, c)
     core_moves[last].wait_recv()
     for one in v_moves:
         one.wait_recv()

time: 54.1 us -> 52.9 us (0.978)
  the two profiles are of different devices: /device:TPU:1 before, /device:TPU:8 now
where the time goes in v4:
time: 52.9 us; the launch traced here: 52.2 us
  Pallas kernels  51.6 us (98%)
  between operations  0.64 us (1%)
    pallas_call x1, Pallas kernels, shards(): pl.pallas_call(fused_kernel, out_shape=outs, in_specs=[ANY] * 10, out_spe...  49.9 us
    pallas_call x1, Pallas kernels, shards(): pl.pallas_call(finish_kernel, out_shape=outs, in_specs=[ANY] * 4, out_spe...  1.69 us

profile of v4, /device:TPU:8, one launch (start us, length us, event | category | flops | bytes accessed | tf_op | source)
XLA Modules:
  0.0 52.2 jit_solution(13687432859254534456)
XLA Ops:
  0.6 49.9 %iteration.1 = (bf16[4,16,256]{2,1,0:T(8,128)(2,1)}, f32[4,16,256]{2,1,0:T(8,128)}, f32[4,16]{1,0:T(4,128)}, f32[4,32,256]{2,1,0:T(8,128)}) custom-call(bf16[4,16,256]{2,1,0:T(8,128)(2,1)} %prices_in.1, f32[4,16]{1,0:T(4,128)} %wages_in.1, f32[4,256]{1,0:T(4,128)} %share_in.1, bf16[4,256,256]{2,1,0:T(8,128)(2,1)} %io_in.1, bf16[4,32,256,256]{3,2,1,0:T(8,128)(2,1)} %blocks.1, ...), custom_call_target="tpu_custom_call" | custom-call | tf_op jit(solution)/shard_map/iteration/pallas_call | solution.py:360
  50.5 1.7 %finish.1 = (bf16[4,16,256]{2,1,0:T(8,128)(2,1)}, f32[4,16,256]{2,1,0:T(8,128)}, f32[4,16]{1,0:T(4,128)}, f32[4,32,256]{2,1,0:T(8,128)}) custom-call(bf16[4,16,256]{2,1,0:T(8,128)(2,1)} %get-tuple-element.8.refs_0_, f32[4,16,256]{2,1,0:T(8,128)} %get-tuple-element.9.refs_1_, f32[4,16]{1,0:T(4,128)} %get-tuple-element.10.refs_2_, ...), custom_call_target="tpu_custom_call" | custom-call | tf_op jit(solution)/shard_map/finish/pallas_call | solution.py:391

commit v5 on v4

--- a/solution.py
+++ b/solution.py
@@ -10,6 +10,7 @@
 BESIDE = (1, 7)
 ORDER = (4, 5, 3, 1, 7, 6, 2, 0)
 CHUNKS = 4
+LEAD = 4
 LOG2E, LN2 = 1.4426950408889634, 0.6931471805599453
 F32 = jnp.float32
 BF16 = jnp.bfloat16
@@ -230,11 +231,15 @@
             dst[k, at_row] = terms[0]
 
     core_moves = []
-    for k in range(NZ):
+
+    def cross(k):
         fill(outgo, k, 1 - c)
         core_moves.append(
             go(outgo.at[k], from_core.at[k], c_s.at[k], c_r.at[k], at(z, y, 1 - c))
         )
+
+    for k in range(LEAD):
+        cross(k)
     tau_moves = [
         go(tau_part, x_in.at[here], x_s.at[d], x_r.at[d], {"ep": (here + d) % size})
         for d in range(1, size)
@@ -264,6 +269,8 @@
         return value
 
     for k in range(NZ - 1):
+        if k + LEAD < NZ:
+            cross(k + LEAD)
         fill(own, k, c)
         core_moves[k].wait_recv()
         d = ORDER[k]

time: 52.9 us -> 52.6 us (level)
  no operation moved by 1% of the time
where the time goes in v5:
time: 52.6 us; the launch traced here: 51.9 us
  Pallas kernels  51.3 us (98%)
  between operations  0.64 us (1%)
    pallas_call x1, Pallas kernels, shards(): pl.pallas_call(fused_kernel, out_shape=outs, in_specs=[ANY] * 10, out_spe...  49.6 us
    pallas_call x1, Pallas kernels, shards(): pl.pallas_call(finish_kernel, out_shape=outs, in_specs=[ANY] * 4, out_spe...  1.69 us

profile of v5, /device:TPU:8, one launch (start us, length us, event | category | flops | bytes accessed | tf_op | source)
XLA Modules:
  0.0 51.9 jit_solution(14459076025658084901)
XLA Ops:
  0.6 49.6 %iteration.1 = (bf16[4,16,256]{2,1,0:T(8,128)(2,1)}, f32[4,16,256]{2,1,0:T(8,128)}, f32[4,16]{1,0:T(4,128)}, f32[4,32,256]{2,1,0:T(8,128)}) custom-call(bf16[4,16,256]{2,1,0:T(8,128)(2,1)} %prices_in.1, f32[4,16]{1,0:T(4,128)} %wages_in.1, f32[4,256]{1,0:T(4,128)} %share_in.1, bf16[4,256,256]{2,1,0:T(8,128)(2,1)} %io_in.1, bf16[4,32,256,256]{3,2,1,0:T(8,128)(2,1)} %blocks.1, ...), custom_call_target="tpu_custom_call" | custom-call | tf_op jit(solution)/shard_map/iteration/pallas_call | solution.py:367
  50.3 1.7 %finish.1 = (bf16[4,16,256]{2,1,0:T(8,128)(2,1)}, f32[4,16,256]{2,1,0:T(8,128)}, f32[4,16]{1,0:T(4,128)}, f32[4,32,256]{2,1,0:T(8,128)}) custom-call(bf16[4,16,256]{2,1,0:T(8,128)(2,1)} %get-tuple-element.8.refs_0_, f32[4,16,256]{2,1,0:T(8,128)} %get-tuple-element.9.refs_1_, f32[4,16]{1,0:T(4,128)} %get-tuple-element.10.refs_2_, ...), custom_call_target="tpu_custom_call" | custom-call | tf_op jit(solution)/shard_map/finish/pallas_call | solution.py:398
